TPU v7x, 256 devices: a whole 4x4x8 slice. The times are simulated.
256 devices in a mesh: pipe: 2 (over core), slab: 8 (over x, z_hi), dp: 16 (over z_lo, y).
Axes of the slice: x: 4, y: 4, z: 8 (z_hi: 2, z_lo: 4; z = z_hi * 4 + z_lo), core: 2. Of those that a mesh axis runs over, the one named last changes fastest.
Arguments:
- saved_inputs: bfloat16 [2, 2, 16, 2, 16, 16, 512], P('pipe', None, 'dp', None, 'slab'), may hold values from -12 to 12
- loss_cotangent: bfloat16 [2, 16, 2, 16, 16, 512], P(None, 'dp', None, 'slab'), may hold values from -3 to 3
- upstream: bfloat16 [16, 2, 16, 16, 512], P('dp', None, 'slab'), may hold values from -3 to 3
- conv_weight: bfloat16 [2, 512, 13824], P('pipe', 'dp'), may hold values from -0.0546875 to 0.0546875
- adagn_table: bfloat16 [2, 1000, 1024], P('pipe'), may hold values from -3 to 3
- timesteps: int32 [3, 16], P(None, 'dp'), may hold values from 0 to 999
- frame_counts: int32 [3, 16], P(None, 'dp'), may hold values from 1 to 2
Outputs:
- input_grads: bfloat16 [2, 2, 16, 2, 16, 16, 512], P('pipe', None, 'dp', None, 'slab')
- weight_grad: float32 [2, 512, 13824], P('pipe', 'dp')
- embed_grad: float32 [2, 2, 16, 1024], P('pipe', None, 'dp')
All inputs are finite; a program needn't handle non-finite values.
Results may differ from a plain program's by a relative error of at most 0.015.
Values may be sent and summed in bfloat16 or wider, within the bound.
A program may use at most 128 MiB of HBM per device.

v0:
```python
import math
import jax
import jax.numpy as jnp
from jax import lax
from jax.sharding import PartitionSpec as P

GROUPS = 32
EPS = 1e-05


def silu_grad(preact):
    sigma = jax.nn.sigmoid(preact)
    return sigma * (1.0 + preact * (1.0 - sigma))


def chunk_group_sums(values, groups_here):
    summed = jnp.sum(values.reshape(-1, values.shape[-1]), axis=0)
    return jnp.sum(summed.reshape(groups_here, -1), axis=1)


def tap_stack(padded, frames, rows, cells_wide):
    slices = []
    for depth_at in range(3):
        for vertical in range(3):
            for across in range(3):
                slices.append(
                    padded[
                        ...,
                        depth_at : depth_at + frames,
                        vertical : vertical + rows,
                        across : across + cells_wide,
                        :,
                    ]
                )
    return jnp.stack(slices, 0)


def local(
    saved_inputs, loss_cotangent, upstream, conv_weight, adagn_table, timesteps, frame_counts
):
    section_index = lax.axis_index("pipe")
    slab_index = lax.axis_index("slab")
    slab_count = lax.axis_size("slab")
    replicas = lax.axis_size("dp")
    inputs = saved_inputs[0, :, 0]
    tick_count, frames, slab_rows, cells_wide, channels = inputs.shape
    height_total = slab_rows * slab_count
    chunk = channels // slab_count
    per_group = channels // GROUPS
    groups_here = chunk // per_group
    step_table = adagn_table[0]
    taps = 27
    weight_local = conv_weight[0].reshape(-1, taps, channels)
    steps_now = lax.dynamic_slice_in_dim(timesteps[:, 0], section_index, tick_count)
    counts_now = lax.dynamic_slice_in_dim(frame_counts[:, 0], section_index, tick_count)
    chunk_start = slab_index * chunk
    weight_cols = lax.dynamic_slice_in_dim(weight_local, chunk_start, chunk, axis=2)
    weight_chunk = lax.all_gather(weight_cols, "dp", axis=0, tiled=True)
    kernel = weight_chunk.reshape(channels, 3, 3, 3, chunk)[:, ::-1, ::-1, ::-1, :]
    kernel = jnp.transpose(kernel, (1, 2, 3, 0, 4))
    inputs_chunk = lax.all_to_all(inputs, "slab", 4, 2, tiled=True)
    weight_norm = 1.0 / math.sqrt(tick_count * replicas * frames * height_total * cells_wide)
    embed_norm = 1.0 / math.sqrt(frames * height_total * cells_wide)

    def full_rows(rows_value):
        return lax.all_gather(rows_value, "slab", axis=1, tiled=True)

    cot_first = jnp.where(section_index == 1, loss_cotangent[0, 0], upstream[0])
    cot_full_first = full_rows(cot_first)
    cot_full_later = full_rows(loss_cotangent[1, 0])
    dx_list = []
    embed_list = []
    hidden_list = []
    cot_list = []
    cot_full = cot_full_first
    for tick_index in range(tick_count):
        steps = steps_now[tick_index]
        count = counts_now[tick_index]
        embedded = lax.dynamic_index_in_dim(step_table, steps, keepdims=False).astype(jnp.float32)
        gain = 1.0 + lax.dynamic_slice_in_dim(embedded, chunk_start, chunk)
        bias = lax.dynamic_slice_in_dim(embedded, channels + chunk_start, chunk)
        mask = (jnp.arange(frames, dtype=jnp.int32) < count).astype(jnp.float32)
        mask_cells = mask[:, None, None, None]
        valid = count.astype(jnp.float32) * float(height_total * cells_wide * per_group)
        values = inputs_chunk[tick_index].astype(jnp.float32)
        masked = values * mask_cells
        mean_g = chunk_group_sums(masked, groups_here) / valid
        var_g = chunk_group_sums(masked * values, groups_here) / valid - mean_g * mean_g
        rstd_g = lax.rsqrt(var_g + EPS)
        mean_c = jnp.repeat(mean_g, per_group)
        rstd_c = jnp.repeat(rstd_g, per_group)
        normed = (values - mean_c) * rstd_c
        preact = normed * gain + bias
        hidden = (jax.nn.silu(preact) * mask_cells).astype(jnp.bfloat16)
        hidden_list.append(hidden)
        upward = lax.conv_general_dilated(
            cot_full[None],
            kernel,
            window_strides=(1, 1, 1),
            padding=((1, 1), (1, 1), (1, 1)),
            dimension_numbers=("NDHWC", "DHWIO", "NDHWC"),
            preferred_element_type=jnp.float32,
        )[0]
        pre_grad = upward * silu_grad(preact) * mask_cells
        dnormed = pre_grad * gain
        sum_a = chunk_group_sums(dnormed, groups_here) / valid
        sum_b = chunk_group_sums(dnormed * normed, groups_here) / valid
        scale_part = jnp.sum(pre_grad * normed, axis=(0, 1, 2))
        shift_part = jnp.sum(pre_grad, axis=(0, 1, 2))
        branch = (
            rstd_c
            * (dnormed - jnp.repeat(sum_a, per_group) - normed * jnp.repeat(sum_b, per_group))
            * mask_cells
        )
        cot_chunk = lax.dynamic_slice_in_dim(cot_full, chunk_start, chunk, axis=3)
        result = (cot_chunk.astype(jnp.float32) + branch).astype(jnp.bfloat16)
        result_full = lax.all_gather(result, "slab", axis=3, tiled=True)
        dx_list.append(
            lax.dynamic_slice_in_dim(result_full, slab_index * slab_rows, slab_rows, axis=1)
        )
        embed_list.append(jnp.stack([scale_part, shift_part]))
        cot_list.append(cot_full)
        if tick_index + 1 < tick_count:
            received = lax.ppermute(result_full, "pipe", [(1, 0)])
            cot_full = jnp.where(section_index == 1, cot_full_later, received)
    embed_all = lax.all_gather(jnp.stack(embed_list), "slab", axis=2, tiled=True)
    embed_grad = embed_all.reshape(tick_count, 2 * channels) * embed_norm
    cot_all = jnp.stack(cot_list)
    hidden_all = jnp.pad(jnp.stack(hidden_list), ((0, 0), (1, 1), (1, 1), (1, 1), (0, 0)))
    hidden_taps = tap_stack(hidden_all, frames, height_total, cells_wide)
    grad_term = jnp.einsum(
        "kfrwo,tkfrwi->oti", cot_all, hidden_taps, preferred_element_type=jnp.float32
    )
    grad_shard = lax.psum_scatter(
        (grad_term * weight_norm).astype(jnp.bfloat16), "dp", scatter_dimension=0, tiled=True
    ).astype(jnp.float32)
    weight_grad = lax.all_gather(grad_shard, "slab", axis=2, tiled=True)
    weight_grad = weight_grad.reshape(weight_grad.shape[0], taps * channels)
    input_grads = jnp.stack(dx_list)[None, :, None]
    return (input_grads, weight_grad[None], embed_grad[None, :, None])


def solution(mesh):
    placed = (
        P("pipe", None, "dp", None, "slab", None, None),
        P(None, "dp", None, "slab", None, None),
        P("dp", None, "slab", None, None),
        P("pipe", "dp", None),
        P("pipe", None, None),
        P(None, "dp"),
        P(None, "dp"),
    )
    return jax.shard_map(
        local,
        mesh=mesh,
        in_specs=placed,
        out_specs=(
            P("pipe", None, "dp", None, "slab", None, None),
            P("pipe", "dp", None),
            P("pipe", None, "dp", None),
        ),
        check_vma=False,
    )
```

profile of v0, /device:TPU:40, one launch (start us, length us, event | category | flops | bytes accessed | tf_op | source)
XLA Modules:
  0.0 773.6 jit_solution(17184056033001340081)
XLA Ops:
  7.3 1.7 reshape_squeeze.3
  8.9 0.1 constant_dynamic-slice_fusion.6
  9.1 0.8 copy.161
  9.9 2.1 copy.156
  12.0 0.7 bitcast_bitcast_fusion
  12.7 1.7 reshape.434
  14.4 10.0 %all-to-all-start = ((bf16[8,2,4096]{2,1,0:T(2,128)(2,1)}), bf16[8,2,4096]{2,1,0:T(2,128)(2,1)S(1)}, u32[]{:S(2)}, u32[]{:S(2)}) async-start(bf16[8,2,4096]{2,1,0:T(2,128)(2,1)} %reshape.434), calls=%async_computation | async-start | bytes 262144 | tf_op jit(solution)/shard_map/all_to_all | solution.py:61
  24.6 0.7 fusion.112
  25.2 0.7 compare_convert_fusion
  25.9 0.6 fusion.111
  26.6 48.0 %all_gather.21 = bf16[2,16,16,512]{3,2,1,0:T(8,128)(2,1)S(1)} all-gather(bf16[2,2,16,512]{3,2,1,0:T(8,128)(2,1)S(1)} %bitcast_select_fusion.1), channel_id=1, replica_groups=mesh['pipe'=2,'slab'=8,'dp'=16] {'slab'}, dimensions={1}, use_global_device_ids=true | all-gather | bytes 589824 | tf_op jit(solution)/shard_map/all_gather | solution.py:66
  74.5 0.6 compare_convert_fusion.1
  78.9 0.3 copy.222
  79.3 0.4 copy.160
  81.1 0.8 dynamic-slice_convert_fusion.1
  81.9 0.7 reshape.435
  82.6 1.3 copy.157
  83.9 0.2 fusion.27
  84.9 17.5 %all-gather.4.cloned.1.call-done = bf16[512,27,64]{2,0,1:T(8,128)(2,1)} async-done(((bf16[32,27,64]{2,0,1:T(8,128)(2,1)}), bf16[512,27,64]{2,0,1:T(8,128)(2,1)}) %all-gather.4.cloned.1.call-update) | async-done | bytes 1769488 | tf_op jit(solution)/shard_map/all_gather | solution.py:58
  102.4 7.6 fusion.20
  110.2 0.2 multiply_reduce_fusion.3
  110.4 0.2 fusion.94
  111.4 0.1 add_convert_fusion.1
  111.6 0.8 copy.165
  112.3 156.0 %all_gather.23 = bf16[2,16,16,512]{2,1,0,3:T(8,128)(2,1)} all-gather(bf16[2,16,16,64]{2,1,0,3:T(8,128)(2,1)S(1)} %copy.165), channel_id=1, replica_groups=mesh['pipe'=2,'slab'=8,'dp'=16] {'slab'}, dimensions={3}, use_global_device_ids=true | all-gather | bytes 589824 | tf_op jit(solution)/shard_map/all_gather | solution.py:117
  268.3 4.4 copy.166
  272.7 1.3 collective-permute-start
  274.1 50.2 %all-gather = bf16[1,1,2,16,16,512]{5,4,3,2,1,0:T(8,128)(2,1)S(1)} all-gather(bf16[1,1,2,2,16,512]{5,4,3,2,1,0:T(8,128)(2,1)S(1)} %slice-done), channel_id=2, replica_groups=mesh['pipe'=2,'slab'=8,'dp'=16] {'slab'}, dimensions={3}, use_global_device_ids=true | all-gather | bytes 589824 | tf_op jit(solution)/shard_map/all_gather | solution.py:66
  325.1 0.3 copy.223
  325.5 0.4 copy.170
  326.0 7.6 fusion.17
  333.8 0.2 fusion.93
  336.3 5.7 fusion
  341.9 0.3 all-gather.6.cloned.1.call-start
  342.3 85.7 %reduce-scatter.2.cloned.1.call-done = bf16[32,27,64]{2,0,1:T(8,128)(2,1)} async-done(((bf16[512,27,64]{2,0,1:T(8,128)(2,1)}), bf16[32,27,64]{2,0,1:T(8,128)(2,1)}) %reduce-scatter.2.cloned.1.call-update) | async-done | bytes 110608 | tf_op jit(solution)/shard_map/reduce_scatter | solution.py:134
  428.0 2.7 copy.209
  431.6 0.2 multiply_reduce_fusion.2
  431.9 0.8 copy.179
  432.7 184.7 %all_gather.25 = bf16[2,16,16,512]{2,1,0,3:T(8,128)(2,1)S(1)} all-gather(bf16[2,16,16,64]{2,1,0,3:T(8,128)(2,1)S(1)} %copy.179), channel_id=1, replica_groups=mesh['pipe'=2,'slab'=8,'dp'=16] {'slab'}, dimensions={3}, use_global_device_ids=true | all-gather | bytes 589824 | tf_op jit(solution)/shard_map/all_gather | solution.py:117
  617.4 0.5 constant_dynamic-slice_fusion
  618.0 0.7 copy.221
  618.8 67.8 %all_gather.27 = f32[2,2,512]{1,0,2:T(2,128)S(1)} all-gather(f32[2,2,64]{1,0,2:T(2,128)S(1)} %copy.211), channel_id=1, replica_groups=mesh['pipe'=2,'slab'=8,'dp'=16] {'slab'}, dimensions={2}, use_global_device_ids=true | all-gather | bytes 9216 | tf_op jit(solution)/shard_map/all_gather | solution.py:126
  686.5 0.2 copy.212
  686.7 0.6 mul.507
  687.4 0.7 maximum_bitcast_fusion.1
  688.0 72.2 %all-gather.6.cloned.1.call-done = f32[32,27,512]{1,0,2:T(8,128)} async-done(((f32[32,27,64]{1,0,2:T(8,128)}), f32[32,27,512]{1,0,2:T(8,128)}) %all-gather.6.cloned.1.call-update) | async-done | bytes 1769488 | tf_op jit(solution)/shard_map/all_gather | solution.py:137
  760.3 5.3 copy.210
  765.5 1.6 broadcast_in_dim_reshape.2
  (108 shorter events, 6.7 us)
Async XLA Ops:
  7.2 17.3 %copy-start.2 = (s32[3,1]{0,1:T(1,128)S(1)}, s32[3,1]{0,1:T(1,128)}, u32[]{:S(2)}) copy-start(s32[3,1]{0,1:T(1,128)} %param.12) | copy-start | bytes 40
  7.2 17.3 %copy-start.3 = (s32[3,1]{0,1:T(1,128)S(1)}, s32[3,1]{0,1:T(1,128)}, u32[]{:S(2)}) copy-start(s32[3,1]{0,1:T(1,128)} %param.13) | copy-start | bytes 40
  7.2 19.4 %copy-start.1 = (bf16[1,2,2,16,512]{4,3,2,1,0:T(8,128)(2,1)S(1)}, bf16[1,2,2,16,512]{4,3,2,1,0:T(8,128)(2,1)}, u32[]{:S(2)}) copy-start(bf16[1,2,2,16,512]{4,3,2,1,0:T(8,128)(2,1)} %param.9) | copy-start | bytes 196612
  7.2 19.4 %copy-start = (bf16[2,1,2,2,16,512]{5,4,3,2,1,0:T(8,128)(2,1)S(1)}, bf16[2,1,2,2,16,512]{5,4,3,2,1,0:T(8,128)(2,1)}, u32[]{:S(2)}) copy-start(bf16[2,1,2,2,16,512]{5,4,3,2,1,0:T(8,128)(2,1)} %param.8) | copy-start | bytes 393220
  7.2 95.2 %all-gather.4.cloned.1.call-start = ((), (), s32[]{:S(2)}) async-start(), calls=%async_computation.2 | async-start | bytes 3760128 | tf_op jit(solution)/shard_map/all_gather | solution.py:58
  9.9 92.5 %copy-start.4 = (pred[8,3]{0,1:T(4,128)(4,1)S(1)}, pred[8,3]{0,1:T(4,128)(4,1)}, u32[]{:S(2)}) copy-start(pred[8,3]{0,1:T(4,128)(4,1)} %constant.79) | copy-start | bytes 76
  14.4 67.5 %all-to-all-start = ((bf16[8,2,4096]{2,1,0:T(2,128)(2,1)}), bf16[8,2,4096]{2,1,0:T(2,128)(2,1)S(1)}, u32[]{:S(2)}, u32[]{:S(2)}) async-start(bf16[8,2,4096]{2,1,0:T(2,128)(2,1)} %reshape.434), calls=%async_computation | async-start | bytes 262144 | tf_op jit(solution)/shard_map/all_to_all | solution.py:61
  24.4 403.6 %reduce-scatter.2.cloned.1.call-start = ((), (), s32[]{:S(2)}) async-start(), calls=%async_computation.3 | async-start | bytes 3760128 | tf_op jit(solution)/shard_map/reduce_scatter | solution.py:134
  110.0 164.1 %slice-start = ((bf16[2,1,2,2,16,512]{5,4,3,2,1,0:T(8,128)(2,1)}), bf16[1,1,2,2,16,512]{5,4,3,2,1,0:T(8,128)(2,1)S(1)}, s32[]{:S(2)}) async-start(bf16[2,1,2,2,16,512]{5,4,3,2,1,0:T(8,128)(2,1)} %param.8), calls=%async_computation.5 | async-start | bytes 131072 | tf_op jit(solution)/shard_map/slice | solution.py:70
  272.7 52.3 %collective-permute-start = (bf16[2,16,16,512]{3,2,1,0:T(8,128)(2,1)S(1)}, bf16[2,16,16,512]{3,2,1,0:T(8,128)(2,1)S(1)}, u32[]{:S(2)}, u32[]{:S(2)}) collective-permute-start(bf16[2,16,16,512]{3,2,1,0:T(8,128)(2,1)S(1)} %copy.166), channel_id=1, source_target_pairs={{128,0},{129,1},{130,2},{131,3},{132,4},{133,5},{134,6},{135,7},{1... | collective-permute-start | bytes 1572872 | tf_op jit(solution)/shard_map/ppermute | solution.py:124
  341.9 418.3 %all-gather.6.cloned.1.call-start = ((), (), s32[]{:S(2)}) async-start(), calls=%async_computation.4 | async-start | bytes 9437184 | tf_op jit(solution)/shard_map/all_gather | solution.py:137
Sparse Core Ops, SparseCore 0:
  10.4 91.9 all-gather.3
  342.1 85.8 reduce-scatter.1
  431.2 329.0 all-gather.5
where the time goes:
time: 774 us
  blocking collectives  507 us (66%)
  waiting for transfers between devices  175 us (23%)
  local copies, waits for them, and re-layouts  34.1 us (4%)
  matrix products  20.9 us (3%)
  between operations  19.2 us (2%)
  starting transfers between devices  11.7 us (2%)
    all_gather x2, blocking collectives, local(): result_full = lax.all_gather(result, 'slab', axis=3, tiled=True)  341 us
    all_gather x2, blocking collectives, full_rows(): return lax.all_gather(rows_value, 'slab', axis=1, tiled=True)  98.1 us
    reduce_scatter x1, waiting for transfers between devices, local(): lax.psum_scatter((grad_term * weight_norm).astype(jnp.bfloat16), 'dp', sc...  85.7 us
    all_gather x1, waiting for transfers between devices, local(): weight_grad = lax.all_gather(grad_shard, 'slab', axis=2, tiled=True)  72.2 us
    all_gather x1, blocking collectives, local(): lax.all_gather(jnp.stack(embed_list), 'slab', axis=2, tiled=True)  67.8 us
    all_gather x1, waiting for transfers between devices, local(): weight_chunk = lax.all_gather(weight_cols, 'dp', axis=0, tiled=True)  17.5 us
  transfers between devices with their start and end apart: 5, of which 3 were waited for; matrix products, arithmetic and copies ran while one was open for 2% of the time, Pallas kernels for 0%

commit v1 on v0

--- a/solution.py
+++ b/solution.py
@@ -134,7 +134,9 @@
     grad_shard = lax.psum_scatter(
         (grad_term * weight_norm).astype(jnp.bfloat16), "dp", scatter_dimension=0, tiled=True
     ).astype(jnp.float32)
-    weight_grad = lax.all_gather(grad_shard, "slab", axis=2, tiled=True)
+    weight_grad = jnp.concatenate(
+        lax.all_to_all(jnp.stack([grad_shard] * lax.axis_size("slab")), "slab", 0, 0), axis=2
+    )
     weight_grad = weight_grad.reshape(weight_grad.shape[0], taps * channels)
     input_grads = jnp.stack(dx_list)[None, :, None]
     return (input_grads, weight_grad[None], embed_grad[None, :, None])

time: 774 us -> 714 us (0.922)
  the two profiles are of different devices: /device:TPU:40 before, /device:TPU:24 now
where the time goes in v1:
time: 714 us; the launch traced here: 710 us
  blocking collectives  495 us (69%)
  waiting for transfers between devices  97 us (14%)
  local copies, waits for them, and re-layouts  38.6 us (5%)
  starting transfers between devices  21.4 us (3%)
  matrix products  20.9 us (3%)
  between operations  19.7 us (3%)
  other arithmetic  17.4 us (2%)
    all_gather x2, blocking collectives, local(): result_full = lax.all_gather(result, 'slab', axis=3, tiled=True)  348 us
    all_gather x2, blocking collectives, full_rows(): return lax.all_gather(rows_value, 'slab', axis=1, tiled=True)  99.7 us
    reduce_scatter x1, waiting for transfers between devices, local(): lax.psum_scatter((grad_term * weight_norm).astype(jnp.bfloat16), 'dp', sc...  82.9 us
    all_gather x1, blocking collectives, local(): lax.all_gather(jnp.stack(embed_list), 'slab', axis=2, tiled=True)  46.8 us
    unnamed x55, local copies, waits for them, and re-layouts  16.8 us
    conv_general_dilated x2, matrix products, local(): lax.conv_general_dilated(cot_full[None], kernel, window_strides=(1, 1, 1)...  15.3 us
  transfers between devices with their start and end apart: 5, of which 2 were waited for; matrix products, arithmetic and copies ran while one was open for 3% of the time, Pallas kernels for 0%

profile of v1, /device:TPU:24, one launch (start us, length us, event | category | flops | bytes accessed | tf_op | source)
XLA Modules:
  0.0 709.7 jit_solution(3732292362774109675)
XLA Ops:
  7.3 1.7 reshape_squeeze.3
  9.1 0.8 copy.219
  9.9 2.1 copy.214
  12.0 0.7 bitcast_bitcast_fusion.1
  12.7 1.7 reshape.440
  14.4 10.9 %all-to-all-start = ((bf16[8,2,4096]{2,1,0:T(2,128)(2,1)}), bf16[8,2,4096]{2,1,0:T(2,128)(2,1)S(1)}, u32[]{:S(2)}, u32[]{:S(2)}) async-start(bf16[8,2,4096]{2,1,0:T(2,128)(2,1)} %reshape.440), calls=%async_computation | async-start | bytes 262144 | tf_op jit(solution)/shard_map/all_to_all | solution.py:61
  25.5 0.7 fusion.112
  26.1 0.7 compare_convert_fusion
  26.8 0.6 fusion.111
  27.5 51.7 %all_gather.18 = bf16[2,16,16,512]{3,2,1,0:T(8,128)(2,1)S(1)} all-gather(bf16[2,2,16,512]{3,2,1,0:T(8,128)(2,1)S(1)} %bitcast_select_fusion.1), channel_id=1, replica_groups=mesh['pipe'=2,'slab'=8,'dp'=16] {'slab'}, dimensions={1}, use_global_device_ids=true | all-gather | bytes 589824 | tf_op jit(solution)/shard_map/all_gather | solution.py:66
  79.2 0.6 compare_convert_fusion.1
  84.0 0.4 copy.218
  85.7 0.8 dynamic-slice_convert_fusion.1
  86.6 0.7 reshape.441
  87.3 1.3 copy.215
  89.6 14.1 %all-gather.3.cloned.1.call-done = bf16[512,27,64]{2,0,1:T(8,128)(2,1)} async-done(((bf16[32,27,64]{2,0,1:T(8,128)(2,1)}), bf16[512,27,64]{2,0,1:T(8,128)(2,1)}) %all-gather.3.cloned.1.call-update) | async-done | bytes 1769488 | tf_op jit(solution)/shard_map/all_gather | solution.py:58
  103.7 7.6 %fusion.20 = f32[2,16,8,3,64]{4,2,3,1,0:T(8,128)S(1)} fusion(bf16[512,3,3,3,64]{4,0,3,2,1:T(8,128)(2,1)} %bitcast.342, bf16[2,16,1,7,2,512]{5,3,4,1,0,2:T(8,128)(2,1)S(1)} %slice.148, bf16[2,16,1,8,3,512]{5,3,4,1,0,2:T(8,128)(2,1)S(1)} %copy.218, pred[8,3]{0,1:T(4,128)(4,1)S(1)} %copy-done.9), kind=kOutput, calls=%fused_computation.44 | convolution fusion | flops 872202240 | bytes 3211288 | tf_op jit(solution)/shard_map/conv_general_dilated | solution.py:96
  111.4 0.8 multiply_reduce_fusion.3
  113.4 0.8 copy.223
  114.2 160.9 %all_gather.20 = bf16[2,16,16,512]{2,1,0,3:T(8,128)(2,1)} all-gather(bf16[2,16,16,64]{2,1,0,3:T(8,128)(2,1)S(1)} %copy.223), channel_id=1, replica_groups=mesh['pipe'=2,'slab'=8,'dp'=16] {'slab'}, dimensions={3}, use_global_device_ids=true | all-gather | bytes 589824 | tf_op jit(solution)/shard_map/all_gather | solution.py:117
  275.1 4.4 copy.224
  279.5 1.3 collective-permute-start
  280.9 47.9 %all-gather = bf16[1,1,2,16,16,512]{5,4,3,2,1,0:T(8,128)(2,1)S(1)} all-gather(bf16[1,1,2,2,16,512]{5,4,3,2,1,0:T(8,128)(2,1)S(1)} %slice-done), channel_id=2, replica_groups=mesh['pipe'=2,'slab'=8,'dp'=16] {'slab'}, dimensions={3}, use_global_device_ids=true | all-gather | bytes 589824 | tf_op jit(solution)/shard_map/all_gather | solution.py:66
  330.1 0.4 copy.228
  330.6 7.6 %fusion.17 = f32[2,16,8,3,64]{4,2,3,1,0:T(8,128)S(1)} fusion(bf16[512,3,3,3,64]{4,0,3,2,1:T(8,128)(2,1)} %bitcast.343, bf16[2,16,1,7,2,512]{5,3,4,1,0,2:T(8,128)(2,1)S(1)} %slice.151, bf16[2,16,1,8,3,512]{5,3,4,1,0,2:T(8,128)(2,1)S(1)} %copy.228, pred[8,3]{0,1:T(4,128)(4,1)S(1)} %copy-done.9), kind=kOutput, calls=%fused_computation.43 | convolution fusion | flops 872202240 | bytes 3211288 | tf_op jit(solution)/shard_map/conv_general_dilated | solution.py:96
  338.4 0.9 fusion.93
  341.6 5.7 fusion
  347.3 82.9 %reduce-scatter.2.cloned.1.call-done = bf16[32,27,64]{2,0,1:T(8,128)(2,1)} async-done(((bf16[512,27,64]{2,0,1:T(8,128)(2,1)}), bf16[32,27,64]{2,0,1:T(8,128)(2,1)}) %reduce-scatter.2.cloned.1.call-update) | async-done | bytes 110608 | tf_op jit(solution)/shard_map/reduce_scatter | solution.py:134
  430.2 1.4 broadcast_bitcast_fusion
  431.6 4.1 reshape.442
  435.7 9.1 %all-to-all-start.1 = ((f32[8,1,55296]{2,1,0:T(1,128)}), f32[8,1,55296]{2,1,0:T(1,128)S(1)}, u32[]{:S(2)}, u32[]{:S(2)}) async-start(f32[8,1,55296]{2,1,0:T(1,128)} %reshape.442), calls=%async_computation.2 | async-start | bytes 3538944 | tf_op jit(solution)/shard_map/all_to_all | solution.py:138
  444.8 0.7 maximum_bitcast_fusion.2
  445.4 0.8 dynamic-slice_bitcast_fusion
  446.3 1.1 fusion.107
  448.1 1.3 multiply_reduce_fusion.2
  449.4 1.1 add_convert_fusion
  450.5 0.8 copy.237
  451.3 187.4 %all_gather.22 = bf16[2,16,16,512]{2,1,0,3:T(8,128)(2,1)S(1)} all-gather(bf16[2,16,16,64]{2,1,0,3:T(8,128)(2,1)S(1)} %copy.237), channel_id=1, replica_groups=mesh['pipe'=2,'slab'=8,'dp'=16] {'slab'}, dimensions={3}, use_global_device_ids=true | all-gather | bytes 589824 | tf_op jit(solution)/shard_map/all_gather | solution.py:117
  638.7 0.5 constant_dynamic-slice_fusion
  639.3 0.7 copy.278
  640.1 46.8 %all_gather.23 = f32[2,2,512]{1,0,2:T(2,128)S(1)} all-gather(f32[2,2,64]{1,0,2:T(2,128)S(1)} %copy.268), channel_id=1, replica_groups=mesh['pipe'=2,'slab'=8,'dp'=16] {'slab'}, dimensions={2}, use_global_device_ids=true | all-gather | bytes 9216 | tf_op jit(solution)/shard_map/all_gather | solution.py:126
  687.0 0.6 mul.507
  687.7 0.7 maximum_bitcast_fusion.1
  688.3 0.6 broadcast.462
  688.9 6.6 reduce.8
  695.6 2.9 reshape.443
  698.8 2.1 copy.267
  700.9 1.8 broadcast_in_dim_reshape_reshape.3
  (122 shorter events, 8.3 us)
Async XLA Ops:
  7.2 18.2 %copy-start.7 = (s32[3,1]{0,1:T(1,128)S(1)}, s32[3,1]{0,1:T(1,128)}, u32[]{:S(2)}) copy-start(s32[3,1]{0,1:T(1,128)} %param.12) | copy-start | bytes 40
  7.2 18.2 %copy-start.8 = (s32[3,1]{0,1:T(1,128)S(1)}, s32[3,1]{0,1:T(1,128)}, u32[]{:S(2)}) copy-start(s32[3,1]{0,1:T(1,128)} %param.13) | copy-start | bytes 40
  7.2 20.3 %copy-start.5 = (bf16[1,2,2,16,512]{4,3,2,1,0:T(8,128)(2,1)S(1)}, bf16[1,2,2,16,512]{4,3,2,1,0:T(8,128)(2,1)}, u32[]{:S(2)}) copy-start(bf16[1,2,2,16,512]{4,3,2,1,0:T(8,128)(2,1)} %param.9) | copy-start | bytes 196612
  7.2 20.3 %copy-start.4 = (bf16[2,1,2,2,16,512]{5,4,3,2,1,0:T(8,128)(2,1)S(1)}, bf16[2,1,2,2,16,512]{5,4,3,2,1,0:T(8,128)(2,1)}, u32[]{:S(2)}) copy-start(bf16[2,1,2,2,16,512]{5,4,3,2,1,0:T(8,128)(2,1)} %param.8) | copy-start | bytes 393220
  7.2 96.5 %all-gather.3.cloned.1.call-start = ((), (), s32[]{:S(2)}) async-start(), calls=%async_computation.3 | async-start | bytes 3760128 | tf_op jit(solution)/shard_map/all_gather | solution.py:58
  9.9 93.8 %copy-start.9 = (pred[8,3]{0,1:T(4,128)(4,1)S(1)}, pred[8,3]{0,1:T(4,128)(4,1)}, u32[]{:S(2)}) copy-start(pred[8,3]{0,1:T(4,128)(4,1)} %constant.79) | copy-start | bytes 76
  14.4 72.2 %all-to-all-start = ((bf16[8,2,4096]{2,1,0:T(2,128)(2,1)}), bf16[8,2,4096]{2,1,0:T(2,128)(2,1)S(1)}, u32[]{:S(2)}, u32[]{:S(2)}) async-start(bf16[8,2,4096]{2,1,0:T(2,128)(2,1)} %reshape.440), calls=%async_computation | async-start | bytes 262144 | tf_op jit(solution)/shard_map/all_to_all | solution.py:61
  25.3 404.9 %reduce-scatter.2.cloned.1.call-start = ((), (), s32[]{:S(2)}) async-start(), calls=%async_computation.4 | async-start | bytes 3760128 | tf_op jit(solution)/shard_map/reduce_scatter | solution.py:134
  89.6 248.8 %copy-start = (f32[1,2,8,2,16,64]{5,4,3,2,1,0:T(8,128)}, f32[1,2,8,2,16,64]{5,4,3,2,1,0:T(8,128)S(1)}, u32[]{:S(2)}) copy-start(f32[1,2,8,2,16,64]{5,4,3,2,1,0:T(8,128)S(1)} %get-tuple-element.45) | copy-start | bytes 393220
  111.3 169.6 %slice-start = ((bf16[2,1,2,2,16,512]{5,4,3,2,1,0:T(8,128)(2,1)}), bf16[1,1,2,2,16,512]{5,4,3,2,1,0:T(8,128)(2,1)S(1)}, s32[]{:S(2)}) async-start(bf16[2,1,2,2,16,512]{5,4,3,2,1,0:T(8,128)(2,1)} %param.8), calls=%async_computation.5 | async-start | bytes 131072 | tf_op jit(solution)/shard_map/slice | solution.py:70
  279.5 50.1 %copy-start.3 = (bf16[2,16,16,512]{3,2,1,0:T(8,128)(2,1)}, bf16[2,16,16,512]{3,2,1,0:T(8,128)(2,1)S(1)}, u32[]{:S(2)}) copy-start(bf16[2,16,16,512]{3,2,1,0:T(8,128)(2,1)S(1)} %copy.224) | copy-start | bytes 1572868
  279.5 50.1 %collective-permute-start = (bf16[2,16,16,512]{3,2,1,0:T(8,128)(2,1)S(1)}, bf16[2,16,16,512]{3,2,1,0:T(8,128)(2,1)S(1)}, u32[]{:S(2)}, u32[]{:S(2)}) collective-permute-start(bf16[2,16,16,512]{3,2,1,0:T(8,128)(2,1)S(1)} %copy.224), channel_id=1, source_target_pairs={{128,0},{129,1},{130,2},{131,3},{132,4},{133,5},{134,6},{135,7},{1... | collective-permute-start | bytes 1572872 | tf_op jit(solution)/shard_map/ppermute | solution.py:124
  280.9 57.5 %copy-start.6 = (f32[64]{0:T(128)}, f32[64]{0:T(128)S(1)}, u32[]{:S(2)}) copy-start(f32[64]{0:T(128)S(1)} %get-tuple-element.49) | copy-start | bytes 772
  329.7 11.9 %copy-start.1 = (bf16[2,16,16,512]{3,2,1,0:T(8,128)(2,1)}, bf16[2,16,16,512]{3,2,1,0:T(8,128)(2,1)S(1)}, u32[]{:S(2)}) copy-start(bf16[2,16,16,512]{3,2,1,0:T(8,128)(2,1)S(1)} %bitcast_select_fusion) | copy-start | bytes 1572868
  338.4 3.1 copy-start.2
  435.7 252.7 %all-to-all-start.1 = ((f32[8,1,55296]{2,1,0:T(1,128)}), f32[8,1,55296]{2,1,0:T(1,128)S(1)}, u32[]{:S(2)}, u32[]{:S(2)}) async-start(f32[8,1,55296]{2,1,0:T(1,128)} %reshape.442), calls=%async_computation.2 | async-start | bytes 3538944 | tf_op jit(solution)/shard_map/all_to_all | solution.py:138
Sparse Core Ops, SparseCore 0:
  10.4 93.2 all-gather.2
  347.4 82.7 reduce-scatter.1
